TPU v7x, 256 devices: a whole 4x4x8 slice. The times are simulated.
256 devices in a mesh: cal: 2 (over x_lo), gr: 16 (over x_hi, y, core), gc: 8 (over z).
Axes of the slice: x: 4 (x_hi: 2, x_lo: 2; x = x_hi * 2 + x_lo), y: 4, z: 8, core: 2. Of those that a mesh axis runs over, the one named last changes fastest.
Arguments:
- tokens: bfloat16 [512, 8192], P(('gr', 'gc'), 'cal'), may hold values from -12 to 12
- gate_weight: bfloat16 [8192, 28672], P(None, ('cal', 'gr', 'gc')), may hold values from -0.0625 to 0.0625
- up_weight: bfloat16 [8192, 28672], P(None, ('cal', 'gr', 'gc')), may hold values from -0.0625 to 0.0625
- hessian_slab: float32 [28672, 8192], P(('cal', 'gr'), 'gc'), may hold values from -1.2 to 1.2
- weight_error: float32 [512, 28672], P(None, ('cal', 'gr')), may hold values from -0.18 to 0.18
- slab_offset: int32 [1], replicated, may hold values from 0 to 20480
- token_count: int32 [1], replicated, may hold values from 512 to 1023
Outputs:
- new_slab: float32 [28672, 8192], P(('cal', 'gr'), 'gc')
- gradient: float32 [512, 8192], P(('cal', 'gr'), 'gc')
Inputs may be any that keep to these rules, and one draw needn't show every extreme that they name: The slab holds the Hessian's columns slab_offset[0] to slab_offset[0] + 8191.
All inputs are finite; a program needn't handle non-finite values.
Results may differ from a plain program's by a relative error of at most 0.0038.
Values may be sent and summed in bfloat16 or wider, within the bound.
No kernel may reach another device: no remote copies, remote signals or barrier semaphores. Data moves between devices by JAX's collectives and lax.ppermute only.
A program may use at most 64 MiB of HBM per device.

v0:
```python
import jax
import jax.numpy as jnp
from jax import lax
from jax.sharding import Mesh
from jax.sharding import PartitionSpec as P

GR_GC = ("gr_0", "gr_1", "gr_2", "gc")
GR = ("gr_0", "gr_1", "gr_2")
CAL_GR = ("cal", "gr_0", "gr_1", "gr_2")
CAL_GR_GC = ("cal", "gr_0", "gr_1", "gr_2", "gc")


def in_blocks(array, dim, devices):
    dims = array.shape
    tiles = array.reshape(*dims[:dim], devices, dims[dim] // devices, *dims[dim + 1 :])
    return jnp.moveaxis(tiles, dim, 0)


def summed_on_arrival(array, axis, dim):
    tiles = in_blocks(array, dim, lax.axis_size(axis))
    arrived = lax.all_to_all(tiles, axis, split_axis=0, concat_axis=0, tiled=True)
    return arrived.sum(axis=0)


def sent_together(arrays, axis, dim, along):
    widths = [a.shape[along] for a in arrays]
    both = jnp.concatenate(arrays, axis=along)
    filled = summed_on_arrival(both, axis, dim)
    return tuple(jnp.split(filled, [sum(widths[:k]) for k in range(1, len(widths))], axis=along))


def joined_along(tiles, dim):
    dims = list(tiles.shape[1:])
    dims[dim] *= tiles.shape[0]
    return jnp.moveaxis(tiles, 0, dim).reshape(dims)


def copy_for_each(array, axis):
    copies = jnp.broadcast_to(array, (lax.axis_size(axis), *array.shape))
    return lax.all_to_all(copies, axis, split_axis=0, concat_axis=0, tiled=True)


def gathered_copies(array, axis, dim):
    return joined_along(copy_for_each(array, axis), dim)


def sum_at_owner(array, axis, dim):
    devices = lax.axis_size(axis)
    tiles = lax.all_to_all(in_blocks(array, dim, devices), axis, 0, 0, tiled=True)
    return jnp.sum(tiles.astype(jnp.float32), axis=0)


def sum_by_axis(array, axes, dim):
    far, near = axes
    own = sum_at_owner(in_blocks(array, dim, lax.axis_size(far)), near, dim + 1)
    return jnp.sum(
        lax.all_to_all(own.astype(jnp.bfloat16), far, 0, 0, tiled=True).astype(jnp.float32), axis=0
    )


def rows_for(lines, devices):
    spare = -len(lines) % devices
    return jnp.pad(lines, [(0, spare)] + [(0, 0)] * (lines.ndim - 1))


def gather_axes(array, axes, dim):
    far, near = axes
    tiles = copy_for_each(copy_for_each(array, far), near)
    return joined_along(tiles.swapaxes(0, 1).reshape(-1, *array.shape), dim)


def total_of(array, axes):
    lines = array.reshape(-1, array.shape[-1])
    own = sum_by_axis(rows_for(lines, lax.axis_size(axes[0]) * lax.axis_size(axes[1])), axes, 0)
    whole = gather_axes(own.astype(jnp.bfloat16), axes, 0)
    return whole[: len(lines)].reshape(array.shape).astype(jnp.float32)


def on_device(tokens, gate_weight, up_weight, hessian_slab, weight_error, slab_offset, token_count):
    token_rows = lax.all_gather(tokens, GR_GC, axis=0, tiled=True)
    sent_gate, sent_up = (
        lax.all_to_all(gate_weight, "cal", split_axis=0, concat_axis=1, tiled=True),
        lax.all_to_all(up_weight, "cal", split_axis=0, concat_axis=1, tiled=True),
    )
    part_gate = jnp.dot(token_rows, sent_gate, preferred_element_type=jnp.float32)
    part_up = jnp.dot(token_rows, sent_up, preferred_element_type=jnp.float32)
    gate_pre, up_pre = sent_together((part_gate, part_up), "cal", 1, 0)
    hidden = (jax.nn.silu(gate_pre) * up_pre).astype(jnp.bfloat16)
    row_panel = gathered_copies(hidden, "gc", 1)
    panel_width = row_panel.shape[1]
    block_width = hessian_slab.shape[1]
    panel_index = lax.axis_index("cal") * lax.axis_size(GR) + lax.axis_index(GR)
    first_col = slab_offset[0] + lax.axis_index("gc") * block_width
    padded = jnp.pad(row_panel, ((0, 0), (block_width, block_width)))
    shifted = jnp.clip(
        first_col - panel_index * panel_width + block_width, 0, panel_width + block_width
    )
    own_share = lax.dynamic_slice_in_dim(padded, shifted, block_width, 1)
    window = total_of(own_share, (("cal", "gr_0", "gr_1"), "gr_2")).astype(jnp.bfloat16)
    gram_block = lax.dot_general(
        row_panel, window, (((0,), (0,)), ((), ())), preferred_element_type=jnp.float32
    )
    new_slab = hessian_slab + gram_block / token_count[0].astype(jnp.float32)
    gradient = summed_on_arrival(
        jnp.dot(
            weight_error,
            new_slab,
            precision=lax.Precision.HIGHEST,
            preferred_element_type=jnp.float32,
        ),
        CAL_GR,
        0,
    )
    return (new_slab, gradient)


def solution(mesh):
    split = Mesh(
        mesh.devices.reshape(mesh.shape["cal"], 2, 4, 2, mesh.shape["gc"]),
        ("cal", "gr_0", "gr_1", "gr_2", "gc"),
    )
    return jax.shard_map(
        on_device,
        mesh=split,
        in_specs=(
            P(GR_GC, "cal"),
            P(None, CAL_GR_GC),
            P(None, CAL_GR_GC),
            P(CAL_GR, "gc"),
            P(None, CAL_GR),
            P(),
            P(),
        ),
        out_specs=(P(CAL_GR, "gc"), P(CAL_GR, "gc")),
        check_vma=False,
    )
```

profile of v0, /device:TPU:1, one launch (start us, length us, event | category | flops | bytes accessed | tf_op | source)
XLA Modules:
  0.0 291.9 jit_solution(8939373543817521909)
XLA Ops:
  7.2 0.0 copy-start
  7.2 0.0 all-gather.3.cloned.1.call-start
  7.2 0.7 all-gather.3.cloned.1.call-update
  7.9 3.0 %copy.27 = bf16[14,2,8,4096]{3,2,0,1:T(8,128)(2,1)} copy(bf16[14,2,8,4096]{3,2,1,0:T(8,128)(2,1)} %bitcast.48) | data formatting | bytes 3670016 | tf_op jit(solution)/shard_map/all_to_all | solution.py:82
  10.9 4.8 %all-to-all-start = ((bf16[2,4096,112]{1,2,0:T(8,128)(2,1)}), bf16[2,4096,112]{1,2,0:T(8,128)(2,1)}, u32[]{:S(2)}, u32[]{:S(2)}) async-start(bf16[2,4096,112]{1,2,0:T(8,128)(2,1)} %bitcast.43), calls=%async_computation | async-start | bytes 3670016 | tf_op jit(solution)/shard_map/all_to_all | solution.py:82
  15.7 2.9 %copy.26 = bf16[14,2,8,4096]{3,2,0,1:T(8,128)(2,1)} copy(bf16[14,2,8,4096]{3,2,1,0:T(8,128)(2,1)} %bitcast.49) | data formatting | bytes 3670016 | tf_op jit(solution)/shard_map/all_to_all | solution.py:83
  18.6 17.3 %all-to-all-done = bf16[2,4096,112]{1,2,0:T(8,128)(2,1)} async-done(((bf16[2,4096,112]{1,2,0:T(8,128)(2,1)}), bf16[2,4096,112]{1,2,0:T(8,128)(2,1)}, u32[]{:S(2)}, u32[]{:S(2)}) %all-to-all-start) | async-done | bytes 1835040 | tf_op jit(solution)/shard_map/all_to_all | solution.py:82
  35.9 4.7 %all-to-all-start.1 = ((bf16[2,4096,112]{1,2,0:T(8,128)(2,1)}), bf16[2,4096,112]{1,2,0:T(8,128)(2,1)}, u32[]{:S(2)}, u32[]{:S(2)}) async-start(bf16[2,4096,112]{1,2,0:T(8,128)(2,1)} %bitcast.42), calls=%async_computation.1 | async-start | bytes 3670016 | tf_op jit(solution)/shard_map/all_to_all | solution.py:83
  40.6 95.0 %all-gather.3.cloned.1.call-done = bf16[128,4,4096]{2,1,0:T(4,128)(2,1)} async-done(((bf16[1,4,4096]{2,1,0:T(4,128)(2,1)}), bf16[128,4,4096]{2,1,0:T(4,128)(2,1)}) %all-gather.3.cloned.1.call-update) | async-done | bytes 4194320 | tf_op jit(solution)/shard_map/all_gather | solution.py:80
  135.7 6.9 %reshape.24 = bf16[512,4096]{1,0:T(8,128)(2,1)} reshape(bf16[128,4,4096]{2,1,0:T(4,128)(2,1)} %all-gather.3.cloned.1.call-done) | data formatting | bytes 8388608
  142.6 4.2 %fusion.1 = f32[512,224]{0,1:T(8,128)S(1)} fusion(bf16[512,4096]{1,0:T(8,128)(2,1)} %reshape.24, bf16[4096,224]{0,1:T(8,128)(2,1)} %bitcast.2), kind=kOutput, calls=%fused_computation.7 | convolution fusion | flops 939524096 | bytes 6488064 | tf_op jit(solution)/shard_map/dot_general | solution.py:85
  146.8 0.0 all-to-all-done.1
  146.8 4.2 %fusion.2 = f32[512,224]{0,1:T(8,128)S(1)} fusion(bf16[512,4096]{1,0:T(8,128)(2,1)} %reshape.24, bf16[4096,224]{0,1:T(8,128)(2,1)} %bitcast.4), kind=kOutput, calls=%fused_computation.8 | convolution fusion | flops 939524096 | bytes 6488064 | tf_op jit(solution)/shard_map/dot_general | solution.py:86
  151.0 0.1 pad_maximum_fusion
  151.1 14.4 %all_to_all.73 = f32[2,1024,112]{1,2,0:T(8,128)S(1)} all-to-all(f32[2,1024,112]{1,2,0:T(8,128)S(1)} %bitcast.47), channel_id=1, replica_groups=mesh['cal'=2,'gr_0'=2,'gr_1'=4,'gr_2'=2,'gc'=8] {'cal'}, dimensions={0} | all-to-all | bytes 1835008 | tf_op jit(solution)/shard_map/all_to_all | solution.py:21
  165.5 0.1 reduce_sum.42
  165.6 0.1 fusion
  165.7 1.0 broadcast_in_dim.9
  166.7 4.1 %all-to-all-start.3 = ((bf16[8,512,112]{1,2,0:T(8,128)(2,1)}), bf16[8,512,112]{1,2,0:T(8,128)(2,1)S(1)}, u32[]{:S(2)}, u32[]{:S(2)}) async-start(bf16[8,512,112]{1,2,0:T(8,128)(2,1)} %broadcast_in_dim.9), calls=%async_computation.3 | async-start | bytes 1835008 | tf_op jit(solution)/shard_map/all_to_all | solution.py:40
  171.4 25.7 %all-to-all-done.3 = bf16[8,512,112]{1,2,0:T(8,128)(2,1)S(1)} async-done(((bf16[8,512,112]{1,2,0:T(8,128)(2,1)}), bf16[8,512,112]{1,2,0:T(8,128)(2,1)S(1)}, u32[]{:S(2)}, u32[]{:S(2)}) %all-to-all-start.3) | async-done | bytes 917536 | tf_op jit(solution)/shard_map/all_to_all | solution.py:40
  197.2 0.0 copy-start.1
  197.2 0.9 copy-done.1
  198.1 0.5 pad_dynamic-slice_fusion
  198.6 1.3 copy.19
  199.9 1.3 copy.20
  201.2 4.7 %all_to_all.74 = bf16[2,16,16,1024]{3,2,1,0:T(8,128)(2,1)S(1)} all-to-all(bf16[2,16,16,1024]{3,2,1,0:T(8,128)(2,1)S(1)} %copy.20), channel_id=1, replica_groups=mesh['cal'=2,'gr_0'=2,'gr_1'=4,'gr_2'=2,'gc'=8] {'gr_2'}, dimensions={0} | all-to-all | bytes 2097152 | tf_op jit(solution)/shard_map/all_to_all | solution.py:49
  205.9 0.3 reduce_sum.43
  206.2 14.7 %all_to_all.75 = bf16[16,16,1024]{2,1,0:T(8,128)(2,1)S(1)} all-to-all(bf16[16,16,1024]{2,1,0:T(8,128)(2,1)S(1)} %reduce_sum.43), channel_id=1, replica_groups=mesh['cal'=2,'gr_0'=2,'gr_1'=4,'gr_2'=2,'gc'=8] {'cal','gr_0','gr_1'}, dimensions={0} | all-to-all | bytes 1048576 | tf_op jit(solution)/shard_map/all_to_all | solution.py:57
  220.9 0.1 reduce_sum.44
  221.0 0.9 broadcast_in_dim.10
  221.9 3.6 %all-to-all-start.6 = ((bf16[16,16,1024]{2,1,0:T(8,128)(2,1)}), bf16[16,16,1024]{2,1,0:T(8,128)(2,1)S(1)}, u32[]{:S(2)}, u32[]{:S(2)}) async-start(bf16[16,16,1024]{2,1,0:T(8,128)(2,1)} %broadcast_in_dim.10), calls=%async_computation.6 | async-start | bytes 1048576 | tf_op jit(solution)/shard_map/all_to_all | solution.py:40
  225.4 0.0 copy-start.2
  226.2 8.3 %all-to-all-done.6 = bf16[16,16,1024]{2,1,0:T(8,128)(2,1)S(1)} async-done(((bf16[16,16,1024]{2,1,0:T(8,128)(2,1)}), bf16[16,16,1024]{2,1,0:T(8,128)(2,1)S(1)}, u32[]{:S(2)}, u32[]{:S(2)}) %all-to-all-start.6) | async-done | bytes 524320 | tf_op jit(solution)/shard_map/all_to_all | solution.py:40
  234.4 0.0 copy-start.4
  234.4 0.1 broadcast_in_dim.11
  234.6 7.8 %all_to_all.76 = bf16[2,16,16,1024]{3,2,1,0:T(8,128)(2,1)S(1)} all-to-all(bf16[2,16,16,1024]{3,2,1,0:T(8,128)(2,1)S(1)} %broadcast_in_dim.11), channel_id=1, replica_groups=mesh['cal'=2,'gr_0'=2,'gr_1'=4,'gr_2'=2,'gc'=8] {'gr_2'}, dimensions={0} | all-to-all | bytes 2097152 | tf_op jit(solution)/shard_map/all_to_all | solution.py:40
  242.4 0.1 copy.21
  242.5 0.0 copy-done.2
  242.5 0.0 copy-done.4
  242.5 1.1 divide_add_fusion
  243.6 0.0 copy-done
  243.6 0.0 copy-start.3
  243.6 6.8 %fusion.3 = f32[1024,512]{0,1:T(8,128)S(1)} fusion(f32[896,1024]{1,0:T(8,128)S(1)} %divide_add_fusion, f32[512,896]{1,0:T(8,128)S(1)} %copy-done), kind=kOutput, calls=%fused_computation.9 | convolution fusion | flops 5637144576 | bytes 7602176 | tf_op jit(solution)/shard_map/dot_general | solution.py:105
  250.4 0.0 copy-done.3
  250.5 32.3 %all_to_all.77 = f32[32,16,1024]{2,1,0:T(8,128)} all-to-all(f32[32,16,1024]{2,1,0:T(8,128)S(1)} %bitcast.41), channel_id=1, replica_groups=mesh['cal'=2,'gr_0'=2,'gr_1'=4,'gr_2'=2,'gc'=8] {'cal','gr_0','gr_1','gr..., dimensions={0} | all-to-all | bytes 4194304 | tf_op jit(solution)/shard_map/all_to_all | solution.py:21
  282.8 2.3 reduce_sum.45
Async XLA Ops:
  7.2 236.4 %copy-start = (f32[512,896]{1,0:T(8,128)S(1)}, f32[512,896]{1,0:T(8,128)}, u32[]{:S(2)}) copy-start(f32[512,896]{1,0:T(8,128)} %param.11) | copy-start | bytes 5505028
  7.2 128.5 %all-gather.3.cloned.1.call-start = ((), (), s32[]{:S(2)}) async-start(), calls=%async_computation.9 | async-start | bytes 4227072 | tf_op jit(solution)/shard_map/all_gather | solution.py:80
  10.9 25.0 %all-to-all-start = ((bf16[2,4096,112]{1,2,0:T(8,128)(2,1)}), bf16[2,4096,112]{1,2,0:T(8,128)(2,1)}, u32[]{:S(2)}, u32[]{:S(2)}) async-start(bf16[2,4096,112]{1,2,0:T(8,128)(2,1)} %bitcast.43), calls=%async_computation | async-start | bytes 3670016 | tf_op jit(solution)/shard_map/all_to_all | solution.py:82
  35.9 110.9 %all-to-all-start.1 = ((bf16[2,4096,112]{1,2,0:T(8,128)(2,1)}), bf16[2,4096,112]{1,2,0:T(8,128)(2,1)}, u32[]{:S(2)}, u32[]{:S(2)}) async-start(bf16[2,4096,112]{1,2,0:T(8,128)(2,1)} %bitcast.42), calls=%async_computation.1 | async-start | bytes 3670016 | tf_op jit(solution)/shard_map/all_to_all | solution.py:83
  166.7 30.5 %all-to-all-start.3 = ((bf16[8,512,112]{1,2,0:T(8,128)(2,1)}), bf16[8,512,112]{1,2,0:T(8,128)(2,1)S(1)}, u32[]{:S(2)}, u32[]{:S(2)}) async-start(bf16[8,512,112]{1,2,0:T(8,128)(2,1)} %broadcast_in_dim.9), calls=%async_computation.3 | async-start | bytes 1835008 | tf_op jit(solution)/shard_map/all_to_all | solution.py:40
  197.2 0.9 copy-start.1
  221.9 12.6 %all-to-all-start.6 = ((bf16[16,16,1024]{2,1,0:T(8,128)(2,1)}), bf16[16,16,1024]{2,1,0:T(8,128)(2,1)S(1)}, u32[]{:S(2)}, u32[]{:S(2)}) async-start(bf16[16,16,1024]{2,1,0:T(8,128)(2,1)} %broadcast_in_dim.10), calls=%async_computation.6 | async-start | bytes 1048576 | tf_op jit(solution)/shard_map/all_to_all | solution.py:40
  225.4 17.0 %copy-start.2 = (bf16[8,512,112]{1,2,0:T(8,128)(2,1)S(1)}, bf16[8,512,112]{1,2,0:T(8,128)(2,1)}, u32[]{:S(2)}) copy-start(bf16[8,512,112]{1,2,0:T(8,128)(2,1)} %copy-done.1) | copy-start | bytes 2752516
  234.4 8.0 %copy-start.4 = (f32[896,1024]{1,0:T(8,128)S(1)}, f32[896,1024]{1,0:T(8,128)}, u32[]{:S(2)}) copy-start(f32[896,1024]{1,0:T(8,128)} %param.10) | copy-start | bytes 11010052
  243.6 6.8 %copy-start.3 = (f32[896,1024]{1,0:T(8,128)}, f32[896,1024]{1,0:T(8,128)S(1)}, u32[]{:S(2)}) copy-start(f32[896,1024]{1,0:T(8,128)S(1)} %divide_add_fusion) | copy-start | bytes 11010052
Sparse Core Ops, SparseCore 0:
  11.7 123.9 all-gather.2
where the time goes:
time: 293 us; the launch traced here: 292 us
  waiting for transfers between devices  147 us (50%)
  blocking collectives  74 us (25%)
  local copies, waits for them, and re-layouts  18.9 us (6%)
  starting transfers between devices  17.2 us (6%)
  matrix products  16.3 us (6%)
  between operations  15.6 us (5%)
    all_gather x1, waiting for transfers between devices, on_device(): token_rows = lax.all_gather(tokens, GR_GC, axis=0, tiled=True)  95 us
    all_to_all x2, blocking collectives, summed_on_arrival(): lax.all_to_all(tiles, axis, split_axis=0, concat_axis=0, tiled=True)  46.7 us
    all_to_all x2, waiting for transfers between devices, copy_for_each(): return lax.all_to_all(copies, axis, split_axis=0, concat_axis=0, tiled=True)  34 us
    all_to_all x1, waiting for transfers between devices, on_device(): lax.all_to_all(gate_weight, 'cal', split_axis=0, concat_axis=1, tiled=True)  17.3 us
    all_to_all x1, blocking collectives, sum_by_axis(): lax.all_to_all(own.astype(jnp.bfloat16), far, 0, 0, tiled=True)  14.7 us
    unnamed x11, local copies, waits for them, and re-layouts  7.88 us
    all_to_all x1, blocking collectives, copy_for_each(): return lax.all_to_all(copies, axis, split_axis=0, concat_axis=0, tiled=True)  7.81 us
    all_to_all x2, starting transfers between devices, copy_for_each(): return lax.all_to_all(copies, axis, split_axis=0, concat_axis=0, tiled=True)  7.67 us
  transfers between devices with their start and end apart: 5, of which 4 were waited for; matrix products, arithmetic and copies ran while one was open for 6% of the time, Pallas kernels for 0%

commit v1 on v0

--- a/solution.py
+++ b/solution.py
@@ -77,7 +77,9 @@
 
 
 def on_device(tokens, gate_weight, up_weight, hessian_slab, weight_error, slab_offset, token_count):
-    token_rows = lax.all_gather(tokens, GR_GC, axis=0, tiled=True)
+    token_rows = jnp.concatenate(
+        lax.all_to_all(jnp.stack([tokens] * lax.axis_size(GR_GC)), GR_GC, 0, 0), axis=0
+    )
     sent_gate, sent_up = (
         lax.all_to_all(gate_weight, "cal", split_axis=0, concat_axis=1, tiled=True),
         lax.all_to_all(up_weight, "cal", split_axis=0, concat_axis=1, tiled=True),

time: 293 us -> 312 us (1.065)
  starting transfers between devices: 17.2 us -> 42.9 us
  blocking collectives: 74 us -> 92.2 us
  waiting for transfers between devices: 147 us -> 133 us
  between operations: 15.6 us -> 2.2 us
    all_gather x1 -> x0, waiting for transfers between devices: 95 us -> none  [on_device(): token_rows = lax.all_gather(tokens, GR_GC, axis=0, tiled=True)]
    all_to_all x1, waiting for transfers between devices: 17.3 us -> 92.1 us  [on_device(): lax.all_to_all(jnp.stack([tokens] * lax.axis_size(GR_GC)), GR_GC, 0, 0)]
    all_to_all x0 -> x1, blocking collectives: none -> 23.4 us  [on_device(): lax.all_to_all(gate_weight, 'cal', split_axis=0, concat_axis=1, tiled=True)]
    all_to_all x1, starting transfers between devices: 4.76 us -> 19.2 us  [on_device(): lax.all_to_all(jnp.stack([tokens] * lax.axis_size(GR_GC)), GR_GC, 0, 0)]
    all_to_all x2, starting transfers between devices: 7.67 us -> 19 us  [copy_for_each(): return lax.all_to_all(copies, axis, split_axis=0, concat_axis=0, tiled=True)]
    reshape x0 -> x1, local copies, waits for them, and re-layouts: none -> 6.95 us  [on_device(): jnp.concatenate(lax.all_to_all(jnp.stack([tokens] * lax.axis_size(GR_GC))...]
    unnamed x11 -> x12, local copies, waits for them, and re-layouts: 7.88 us -> 0.94 us
    all_to_all x1, waiting for transfers between devices: 0.01 us -> 6.51 us  [on_device(): lax.all_to_all(up_weight, 'cal', split_axis=0, concat_axis=1, tiled=True)]
  transfers between devices with their start and end apart: 5 -> 4, of which waited for: 4 -> 4; matrix products, arithmetic and copies ran while one was open for 6% -> 5% of each run, Pallas kernels for 0% -> 0%
where the time goes in v1:
time: 312 us; the launch traced here: 311 us
  waiting for transfers between devices  133 us (43%)
  blocking collectives  92.2 us (30%)
  starting transfers between devices  42.9 us (14%)
  local copies, waits for them, and re-layouts  21.8 us (7%)
  matrix products  16.3 us (5%)
    all_to_all x1, waiting for transfers between devices, on_device(): lax.all_to_all(jnp.stack([tokens] * lax.axis_size(GR_GC)), GR_GC, 0, 0)  92.1 us
    all_to_all x2, blocking collectives, summed_on_arrival(): lax.all_to_all(tiles, axis, split_axis=0, concat_axis=0, tiled=True)  42.3 us
    all_to_all x2, waiting for transfers between devices, copy_for_each(): return lax.all_to_all(copies, axis, split_axis=0, concat_axis=0, tiled=True)  34 us
    all_to_all x1, blocking collectives, on_device(): lax.all_to_all(gate_weight, 'cal', split_axis=0, concat_axis=1, tiled=True)  23.4 us
    all_to_all x1, starting transfers between devices, on_device(): lax.all_to_all(jnp.stack([tokens] * lax.axis_size(GR_GC)), GR_GC, 0, 0)  19.2 us
    all_to_all x2, starting transfers between devices, copy_for_each(): return lax.all_to_all(copies, axis, split_axis=0, concat_axis=0, tiled=True)  19 us
    all_to_all x1, blocking collectives, sum_by_axis(): lax.all_to_all(own.astype(jnp.bfloat16), far, 0, 0, tiled=True)  14.1 us
    all_to_all x1, blocking collectives, copy_for_each(): return lax.all_to_all(copies, axis, split_axis=0, concat_axis=0, tiled=True)  7.81 us
  transfers between devices with their start and end apart: 4, of which 4 were waited for; matrix products, arithmetic and copies ran while one was open for 5% of the time, Pallas kernels for 0%

profile of v1, /device:TPU:1, one launch (start us, length us, event | category | flops | bytes accessed | tf_op | source)
XLA Modules:
  0.0 310.9 jit_solution(12507016339780444356)
XLA Ops:
  0.6 0.0 copy-start
  0.6 0.0 copy-start.4
  0.7 1.8 copy.27
  2.4 23.4 %all_to_all.78 = bf16[2,4096,112]{1,2,0:T(8,128)(2,1)} all-to-all(bf16[2,4096,112]{1,2,0:T(8,128)(2,1)S(1)} %bitcast.42), channel_id=1, replica_groups=mesh['cal'=2,'gr_0'=2,'gr_1'=4,'gr_2'=2,'gc'=8] {'cal'}, dimensions={0} | all-to-all | bytes 3670016 | tf_op jit(solution)/shard_map/all_to_all | solution.py:84
  25.8 0.0 copy-done.4
  25.8 4.1 %stack.2 = bf16[128,4,4096]{2,1,0:T(4,128)(2,1)} broadcast(bf16[4,4096]{1,0:T(4,128)(2,1)S(1)} %copy-done.4), dimensions={1,2} | broadcast | bytes 4227072 | tf_op jit(solution)/shard_map/stack | solution.py:81
  29.8 19.2 %all-to-all-start = ((bf16[128,4,4096]{2,1,0:T(4,128)(2,1)}), bf16[128,4,4096]{2,1,0:T(4,128)(2,1)}, u32[]{:S(2)}, u32[]{:S(2)}) async-start(bf16[128,4,4096]{2,1,0:T(4,128)(2,1)} %stack.2), calls=%async_computation | async-start | bytes 8388608 | tf_op jit(solution)/shard_map/all_to_all | solution.py:81
  49.0 2.9 copy.26
  52.0 92.1 %all-to-all-done = bf16[128,4,4096]{2,1,0:T(4,128)(2,1)} async-done(((bf16[128,4,4096]{2,1,0:T(4,128)(2,1)}), bf16[128,4,4096]{2,1,0:T(4,128)(2,1)}, u32[]{:S(2)}, u32[]{:S(2)}) %all-to-all-start) | async-done | bytes 4194336 | tf_op jit(solution)/shard_map/all_to_all | solution.py:81
  144.1 4.7 %all-to-all-start.2 = ((bf16[2,4096,112]{1,2,0:T(8,128)(2,1)}), bf16[2,4096,112]{1,2,0:T(8,128)(2,1)}, u32[]{:S(2)}, u32[]{:S(2)}) async-start(bf16[2,4096,112]{1,2,0:T(8,128)(2,1)} %bitcast.41), calls=%async_computation.2 | async-start | bytes 3670016 | tf_op jit(solution)/shard_map/all_to_all | solution.py:85
  148.8 6.9 %reshape.25 = bf16[512,4096]{1,0:T(8,128)(2,1)} reshape(bf16[128,4,4096]{2,1,0:T(4,128)(2,1)} %all-to-all-done) | data formatting | bytes 8388608 | tf_op jit(solution)/shard_map/reshape | solution.py:80
  155.7 4.2 %fusion.1 = f32[512,224]{0,1:T(8,128)S(1)} fusion(bf16[512,4096]{1,0:T(8,128)(2,1)} %reshape.25, bf16[4096,224]{0,1:T(8,128)(2,1)} %bitcast.49), kind=kOutput, calls=%fused_computation.7 | convolution fusion | flops 939524096 | bytes 6488064 | tf_op jit(solution)/shard_map/dot_general | solution.py:87
  159.9 6.5 %all-to-all-done.2 = bf16[2,4096,112]{1,2,0:T(8,128)(2,1)} async-done(((bf16[2,4096,112]{1,2,0:T(8,128)(2,1)}), bf16[2,4096,112]{1,2,0:T(8,128)(2,1)}, u32[]{:S(2)}, u32[]{:S(2)}) %all-to-all-start.2) | async-done | bytes 1835040 | tf_op jit(solution)/shard_map/all_to_all | solution.py:85
  166.5 4.2 %fusion.2 = f32[512,224]{0,1:T(8,128)S(1)} fusion(bf16[512,4096]{1,0:T(8,128)(2,1)} %reshape.25, bf16[4096,224]{0,1:T(8,128)(2,1)} %bitcast.3), kind=kOutput, calls=%fused_computation.8 | convolution fusion | flops 939524096 | bytes 6488064 | tf_op jit(solution)/shard_map/dot_general | solution.py:88
  170.7 0.1 pad_maximum_fusion
  170.7 10.0 %all_to_all.79 = f32[2,1024,112]{1,2,0:T(8,128)S(1)} all-to-all(f32[2,1024,112]{1,2,0:T(8,128)S(1)} %bitcast.46), channel_id=1, replica_groups=mesh['cal'=2,'gr_0'=2,'gr_1'=4,'gr_2'=2,'gc'=8] {'cal'}, dimensions={0} | all-to-all | bytes 1835008 | tf_op jit(solution)/shard_map/all_to_all | solution.py:21
  180.7 0.1 reduce_sum.42
  180.8 0.1 fusion
  180.9 1.0 broadcast_in_dim.9
  181.9 15.4 %all-to-all-start.4 = ((bf16[8,512,112]{1,2,0:T(8,128)(2,1)}), bf16[8,512,112]{1,2,0:T(8,128)(2,1)S(1)}, u32[]{:S(2)}, u32[]{:S(2)}) async-start(bf16[8,512,112]{1,2,0:T(8,128)(2,1)} %broadcast_in_dim.9), calls=%async_computation.4 | async-start | bytes 1835008 | tf_op jit(solution)/shard_map/all_to_all | solution.py:40
  198.0 25.7 %all-to-all-done.4 = bf16[8,512,112]{1,2,0:T(8,128)(2,1)S(1)} async-done(((bf16[8,512,112]{1,2,0:T(8,128)(2,1)}), bf16[8,512,112]{1,2,0:T(8,128)(2,1)S(1)}, u32[]{:S(2)}, u32[]{:S(2)}) %all-to-all-start.4) | async-done | bytes 917536 | tf_op jit(solution)/shard_map/all_to_all | solution.py:40
  223.7 0.0 copy-start.1
  223.7 0.9 copy-done.1
  224.6 0.5 pad_dynamic-slice_fusion
  225.1 1.3 copy.19
  226.4 1.3 copy.20
  227.7 4.7 %all_to_all.80 = bf16[2,16,16,1024]{3,2,1,0:T(8,128)(2,1)S(1)} all-to-all(bf16[2,16,16,1024]{3,2,1,0:T(8,128)(2,1)S(1)} %copy.20), channel_id=1, replica_groups=mesh['cal'=2,'gr_0'=2,'gr_1'=4,'gr_2'=2,'gc'=8] {'gr_2'}, dimensions={0} | all-to-all | bytes 2097152 | tf_op jit(solution)/shard_map/all_to_all | solution.py:49
  232.4 0.3 reduce_sum.43
  232.7 14.1 %all_to_all.81 = bf16[16,16,1024]{2,1,0:T(8,128)(2,1)S(1)} all-to-all(bf16[16,16,1024]{2,1,0:T(8,128)(2,1)S(1)} %reduce_sum.43), channel_id=1, replica_groups=mesh['cal'=2,'gr_0'=2,'gr_1'=4,'gr_2'=2,'gc'=8] {'cal','gr_0','gr_1'}, dimensions={0} | all-to-all | bytes 1048576 | tf_op jit(solution)/shard_map/all_to_all | solution.py:57
  246.8 0.1 reduce_sum.44
  246.8 0.9 broadcast_in_dim.10
  247.7 3.6 %all-to-all-start.7 = ((bf16[16,16,1024]{2,1,0:T(8,128)(2,1)}), bf16[16,16,1024]{2,1,0:T(8,128)(2,1)S(1)}, u32[]{:S(2)}, u32[]{:S(2)}) async-start(bf16[16,16,1024]{2,1,0:T(8,128)(2,1)} %broadcast_in_dim.10), calls=%async_computation.7 | async-start | bytes 1048576 | tf_op jit(solution)/shard_map/all_to_all | solution.py:40
  251.3 0.0 copy-start.2
  252.0 8.3 %all-to-all-done.7 = bf16[16,16,1024]{2,1,0:T(8,128)(2,1)S(1)} async-done(((bf16[16,16,1024]{2,1,0:T(8,128)(2,1)}), bf16[16,16,1024]{2,1,0:T(8,128)(2,1)S(1)}, u32[]{:S(2)}, u32[]{:S(2)}) %all-to-all-start.7) | async-done | bytes 524320 | tf_op jit(solution)/shard_map/all_to_all | solution.py:40
  260.3 0.0 copy-start.5
  260.3 0.1 broadcast_in_dim.11
  260.4 7.8 %all_to_all.82 = bf16[2,16,16,1024]{3,2,1,0:T(8,128)(2,1)S(1)} all-to-all(bf16[2,16,16,1024]{3,2,1,0:T(8,128)(2,1)S(1)} %broadcast_in_dim.11), channel_id=1, replica_groups=mesh['cal'=2,'gr_0'=2,'gr_1'=4,'gr_2'=2,'gc'=8] {'gr_2'}, dimensions={0} | all-to-all | bytes 2097152 | tf_op jit(solution)/shard_map/all_to_all | solution.py:40
  268.2 0.1 copy.21
  268.3 0.0 copy-done.2
  268.3 0.0 copy-done.5
  268.3 1.1 divide_add_fusion
  269.5 0.0 copy-done
  269.5 0.0 copy-start.3
  269.5 6.8 %fusion.3 = f32[1024,512]{0,1:T(8,128)S(1)} fusion(f32[896,1024]{1,0:T(8,128)S(1)} %divide_add_fusion, f32[512,896]{1,0:T(8,128)S(1)} %copy-done), kind=kOutput, calls=%fused_computation.9 | convolution fusion | flops 5637144576 | bytes 7602176 | tf_op jit(solution)/shard_map/dot_general | solution.py:107
  276.3 0.0 copy-done.3
  276.3 32.3 %all_to_all.83 = f32[32,16,1024]{2,1,0:T(8,128)} all-to-all(f32[32,16,1024]{2,1,0:T(8,128)S(1)} %bitcast.40), channel_id=1, replica_groups=mesh['cal'=2,'gr_0'=2,'gr_1'=4,'gr_2'=2,'gc'=8] {'cal','gr_0','gr_1','gr..., dimensions={0} | all-to-all | bytes 4194304 | tf_op jit(solution)/shard_map/all_to_all | solution.py:21
  308.6 2.3 reduce_sum.45
Async XLA Ops:
  0.6 268.8 %copy-start = (f32[512,896]{1,0:T(8,128)S(1)}, f32[512,896]{1,0:T(8,128)}, u32[]{:S(2)}) copy-start(f32[512,896]{1,0:T(8,128)} %param.11) | copy-start | bytes 5505028
  0.6 25.1 %copy-start.4 = (bf16[4,4096]{1,0:T(4,128)(2,1)S(1)}, bf16[4,4096]{1,0:T(4,128)(2,1)}, u32[]{:S(2)}) copy-start(bf16[4,4096]{1,0:T(4,128)(2,1)} %param.7) | copy-start | bytes 98308
  29.8 114.2 %all-to-all-start = ((bf16[128,4,4096]{2,1,0:T(4,128)(2,1)}), bf16[128,4,4096]{2,1,0:T(4,128)(2,1)}, u32[]{:S(2)}, u32[]{:S(2)}) async-start(bf16[128,4,4096]{2,1,0:T(4,128)(2,1)} %stack.2), calls=%async_computation | async-start | bytes 8388608 | tf_op jit(solution)/shard_map/all_to_all | solution.py:81
  144.1 22.4 %all-to-all-start.2 = ((bf16[2,4096,112]{1,2,0:T(8,128)(2,1)}), bf16[2,4096,112]{1,2,0:T(8,128)(2,1)}, u32[]{:S(2)}, u32[]{:S(2)}) async-start(bf16[2,4096,112]{1,2,0:T(8,128)(2,1)} %bitcast.41), calls=%async_computation.2 | async-start | bytes 3670016 | tf_op jit(solution)/shard_map/all_to_all | solution.py:85
  181.9 41.8 %all-to-all-start.4 = ((bf16[8,512,112]{1,2,0:T(8,128)(2,1)}), bf16[8,512,112]{1,2,0:T(8,128)(2,1)S(1)}, u32[]{:S(2)}, u32[]{:S(2)}) async-start(bf16[8,512,112]{1,2,0:T(8,128)(2,1)} %broadcast_in_dim.9), calls=%async_computation.4 | async-start | bytes 1835008 | tf_op jit(solution)/shard_map/all_to_all | solution.py:40
  223.7 0.9 copy-start.1
  247.7 12.6 %all-to-all-start.7 = ((bf16[16,16,1024]{2,1,0:T(8,128)(2,1)}), bf16[16,16,1024]{2,1,0:T(8,128)(2,1)S(1)}, u32[]{:S(2)}, u32[]{:S(2)}) async-start(bf16[16,16,1024]{2,1,0:T(8,128)(2,1)} %broadcast_in_dim.10), calls=%async_computation.7 | async-start | bytes 1048576 | tf_op jit(solution)/shard_map/all_to_all | solution.py:40
  251.3 17.0 %copy-start.2 = (bf16[8,512,112]{1,2,0:T(8,128)(2,1)S(1)}, bf16[8,512,112]{1,2,0:T(8,128)(2,1)}, u32[]{:S(2)}) copy-start(bf16[8,512,112]{1,2,0:T(8,128)(2,1)} %copy-done.1) | copy-start | bytes 2752516
  260.3 8.0 %copy-start.5 = (f32[896,1024]{1,0:T(8,128)S(1)}, f32[896,1024]{1,0:T(8,128)}, u32[]{:S(2)}) copy-start(f32[896,1024]{1,0:T(8,128)} %param.10) | copy-start | bytes 11010052
  269.5 6.8 %copy-start.3 = (f32[896,1024]{1,0:T(8,128)}, f32[896,1024]{1,0:T(8,128)S(1)}, u32[]{:S(2)}) copy-start(f32[896,1024]{1,0:T(8,128)S(1)} %divide_add_fusion) | copy-start | bytes 11010052
